TPU v7x, 256 devices: a whole 4x4x8 slice. The times are simulated.
256 devices in a mesh: facet: 16 (over y, x_lo, core), team: 8 (over z), sub: 2 (over x_hi).
Axes of the slice: x: 4 (x_hi: 2, x_lo: 2; x = x_hi * 2 + x_lo), y: 4, z: 8, core: 2. Of those that a mesh axis runs over, the one named last changes fastest.
Arguments:
- facet_rows: bfloat16 [16, 2, 64, 4096], P('facet', None, 'team'), may hold values from -6 to 6
- sub_offsets: int32 [32, 2], replicated, may hold values from 0 to 4095
- facet_offsets: int32 [16, 2], replicated, may hold values from 0 to 4095
- aterm: bfloat16 [16, 2, 256, 256], P('facet'), may hold values from 0.29882812 to 3
- cells: int32 [16, 2, 8, 2, 256], P('facet', None, 'team'), may hold values from 0 to 1023
- observed: bfloat16 [16, 2, 8, 2, 256], P('facet', None, 'team'), may hold values from -6 to 6
- weights: bfloat16 [16, 2, 8, 256], P('facet', None, 'team'), may hold values from 0.29882812 to 3
- counts: int32 [16, 2, 8], replicated, may hold values from 1 to 256, as said below
Outputs:
- facet_update: float32 [16, 2, 64, 4096], P('facet', None, 'team', 'sub')
Inputs may be any that keep to these rules, and one draw needn't show every extreme that they name: Slots 0 to counts[a, b, t] - 1 are live. For every a and t one of the two subgrids with indices [a, 0] and [a, 1] has at most 64 live slots, and which of the two it is does not change with t.
All inputs are finite; a program needn't handle non-finite values.
Results may differ from a plain program's by a relative error of at most 0.019.
Values may be sent and summed in bfloat16 or wider, within the bound.
No kernel may reach another device: no remote copies, remote signals or barrier semaphores. Data moves between devices by JAX's collectives and lax.ppermute only.
A program may use at most 64 MiB of HBM per device.

v0:
```python
import math
import jax
import jax.numpy as jnp
from jax import lax
from jax.sharding import PartitionSpec as P

L = 4096
M = 128
SG = 256
VB = 256
TWO_PI = 2.0 * math.pi
HIGHEST = lax.Precision.HIGHEST


def cut_along(shard, dim, peers):
    before, after = (shard.shape[:dim], shard.shape[dim + 1 :])
    return jnp.moveaxis(shard.reshape(*before, peers, -1, *after), dim, 0)


def sum_at_owner(shard, axis, dim):
    peers = lax.axis_size(axis)
    parts = lax.all_to_all(cut_along(shard, dim, peers), axis, 0, 0, tiled=True)
    return jnp.sum(parts, axis=0)


def in_order(parts, dim):
    parts = jnp.moveaxis(parts, 0, dim)
    lengths = parts.shape
    return parts.reshape(*lengths[:dim], lengths[dim] * lengths[dim + 1], *lengths[dim + 2 :])


def from_everyone(shard, axis):
    copies = jnp.broadcast_to(shard, (lax.axis_size(axis), *shard.shape))
    return lax.all_to_all(copies, axis, split_axis=0, concat_axis=0, tiled=True)


def collect(shard, axis, dim):
    return in_order(from_everyone(shard, axis), dim)


def over_copies(shard, axis):
    return from_everyone(shard, axis).astype(jnp.float32).sum(axis=0)


def partner(value, axis, stride):
    mask = 2**stride
    pairs = [(source, source ^ mask) for source in range(lax.axis_size(axis))]
    return lax.ppermute(value, axis, pairs)


def angles(left_ints, right_ints, period):
    return (left_ints * right_ints % period).astype(jnp.float32) * (TWO_PI / period)


def transform_tables():
    columns = jnp.arange(L, dtype=jnp.int32)
    frequency = jnp.arange(M, dtype=jnp.int32)
    angle_grid = angles(columns[:, None], frequency[None, :], L)
    cos_part = jnp.cos(angle_grid)
    sin_part = jnp.sin(angle_grid)
    spec_re = (cos_part / math.sqrt(L)).astype(jnp.bfloat16)
    spec_im = (-sin_part / math.sqrt(L)).astype(jnp.bfloat16)
    forward = jnp.concatenate(
        [jnp.concatenate([spec_re, spec_im], 1), jnp.concatenate([-spec_im, spec_re], 1)], 0
    )
    back_re = (cos_part.T / math.sqrt(M)).astype(jnp.bfloat16)
    back_im = (sin_part.T / math.sqrt(M)).astype(jnp.bfloat16)
    backward = jnp.concatenate(
        [jnp.concatenate([back_re, back_im], 1), jnp.concatenate([-back_im, back_re], 1)], 0
    )
    return (forward, backward)


def subgrid_table(size_sub):
    freq_ids = jnp.arange(M, dtype=jnp.int32)
    cell_ids = jnp.arange(size_sub, dtype=jnp.int32)
    angle_grid = angles(freq_ids[:, None], cell_ids[None, :], size_sub)
    factor = 1.0 / math.sqrt(M)
    return (jnp.cos(angle_grid) * factor, jnp.sin(angle_grid) * factor)


def facet_phase(row_ids, facet_offsets):
    col_ids = jnp.arange(M, dtype=jnp.int32)
    along_rows = row_ids[:, None] * facet_offsets[None, :, 0] % L
    along_cols = col_ids[None, :] * facet_offsets[:, 1:2] % L
    angle_grid = ((along_rows[:, :, None] + along_cols[None, :, :]) % L).astype(jnp.float32) * (
        TWO_PI / L
    )
    return (jnp.cos(angle_grid), jnp.sin(angle_grid))


def hdot(left, right):
    return jnp.dot(left, right, precision=HIGHEST, preferred_element_type=jnp.float32)


def hsum(form, left, right):
    return jnp.einsum(form, left, right, precision=HIGHEST, preferred_element_type=jnp.float32)


def to_image(assembled, k_re, k_im):
    grid_re = assembled[:, 0]
    grid_im = assembled[:, 1]
    temp_re = hdot(k_re.T, grid_re) - hdot(k_im.T, grid_im)
    temp_im = hdot(k_re.T, grid_im) + hdot(k_im.T, grid_re)
    image_re = hdot(temp_re, k_re) - hdot(temp_im, k_im)
    image_im = hdot(temp_re, k_im) + hdot(temp_im, k_re)
    return (image_re, image_im)


def to_return(grid, weight_map, k_re, k_im):
    size_sub = weight_map.shape[0]
    grid_re = grid[:, :size_sub] * weight_map / size_sub
    grid_im = grid[:, size_sub:] * weight_map / size_sub
    temp_re = hdot(k_re, grid_re) + hdot(k_im, grid_im)
    temp_im = hdot(k_re, grid_im) - hdot(k_im, grid_re)
    out_re = hdot(temp_re, k_re.T) + hdot(temp_im, k_im.T)
    out_im = hdot(temp_im, k_re.T) - hdot(temp_re, k_im.T)
    return jnp.stack([out_re, out_im], 1)


def degrid_block(weighted, cell_pair, observed_pair, weight, live):
    size_sub = weighted.shape[1]
    block_len = cell_pair.shape[1]
    index = jnp.arange(size_sub, dtype=jnp.int32)
    row_angle = angles(cell_pair[0][:, None], index[None, :], 4 * size_sub)
    col_angle = angles(cell_pair[1][:, None], index[None, :], 4 * size_sub)
    row_cos = jnp.cos(row_angle).astype(jnp.bfloat16)
    row_sin = jnp.sin(row_angle).astype(jnp.bfloat16)
    col_cos = jnp.cos(col_angle).astype(jnp.bfloat16)
    col_sin = jnp.sin(col_angle).astype(jnp.bfloat16)
    col_stack = jnp.concatenate([col_cos, col_sin], 0)
    products = jnp.einsum("jk,ik->ji", col_stack, weighted, preferred_element_type=jnp.float32)
    part_re = products[:block_len, :size_sub] + products[block_len:, size_sub:]
    part_im = products[:block_len, size_sub:] - products[block_len:, :size_sub]
    cos_rows = row_cos.astype(jnp.float32)
    sin_rows = row_sin.astype(jnp.float32)
    cos_cols = col_cos.astype(jnp.float32)
    sin_cols = col_sin.astype(jnp.float32)
    pred_re = jnp.sum(cos_rows * part_re + sin_rows * part_im, 1) / size_sub
    pred_im = jnp.sum(cos_rows * part_im - sin_rows * part_re, 1) / size_sub
    res_re = live * weight * (observed_pair[0] - pred_re)
    res_im = live * weight * (observed_pair[1] - pred_im)
    spread_re = (res_re[:, None] * cos_cols - res_im[:, None] * sin_cols).astype(jnp.bfloat16)
    spread_im = (res_re[:, None] * sin_cols + res_im[:, None] * cos_cols).astype(jnp.bfloat16)
    right = jnp.concatenate(
        [jnp.concatenate([spread_re, spread_im], 1), jnp.concatenate([-spread_im, spread_re], 1)], 0
    )
    left = jnp.concatenate([row_cos, row_sin], 0)
    return jnp.einsum("ji,jk->ik", left, right, preferred_element_type=jnp.float32)


def weigh_image(assembled, weight_map, k_re, k_im):
    image_re, image_im = to_image(assembled, k_re, k_im)
    return jnp.concatenate(
        [
            (weight_map * image_re).astype(jnp.bfloat16),
            (weight_map * image_im).astype(jnp.bfloat16),
        ],
        0,
    )


def local(facet_rows, sub_offsets, facet_offsets, aterm, cells, observed, weights, counts):
    n_facet = lax.axis_size("facet")
    n_team = lax.axis_size("team")
    n_sub = lax.axis_size("sub")
    my_facet = lax.axis_index("facet")
    my_team = lax.axis_index("team")
    my_side = lax.axis_index("sub")
    rows_dev = facet_rows.shape[2]
    rows_all = rows_dev * n_team
    norm = 1.0 / math.sqrt(n_facet)
    share = M // n_team
    forward, backward = transform_tables()
    k_re, k_im = subgrid_table(SG)
    sub_ids = jnp.arange(n_facet, dtype=jnp.int32) * n_sub + my_side
    shifts = sub_offsets[sub_ids, 0]
    tunings = sub_offsets[sub_ids, 1]
    columns = jnp.arange(L, dtype=jnp.int32)
    mod_angle = angles(tunings[:, None], columns[None, :], L)
    mod_cos = jnp.cos(mod_angle)[:, None, :]
    mod_sin = jnp.sin(mod_angle)[:, None, :]
    rows_re = facet_rows[0, 0].astype(jnp.float32)[None]
    rows_im = facet_rows[0, 1].astype(jnp.float32)[None]
    mod_re = (rows_re * mod_cos + rows_im * mod_sin).astype(jnp.bfloat16)
    mod_im = (rows_im * mod_cos - rows_re * mod_sin).astype(jnp.bfloat16)
    stacked = jnp.concatenate([mod_re, mod_im], 2).reshape(n_facet * rows_dev, 2 * L)
    spectrum = jnp.dot(stacked, forward, preferred_element_type=jnp.float32).reshape(
        n_facet, rows_dev, 2, M
    )
    row_ids = my_team * rows_dev + jnp.arange(rows_dev, dtype=jnp.int32)
    out_ids = jnp.arange(M, dtype=jnp.int32)
    w_angle = angles(
        out_ids[None, :, None] + shifts[:, None, None], row_ids[None, None, :], rows_all
    )
    w_re = jnp.cos(w_angle) / math.sqrt(rows_all)
    w_im = -jnp.sin(w_angle) / math.sqrt(rows_all)
    part_re = w_re
    part_im = w_im
    real_out = hsum("fpr,frm->pfm", part_re, spectrum[:, :, 0]) - hsum(
        "fpr,frm->pfm", part_im, spectrum[:, :, 1]
    )
    imag_out = hsum("fpr,frm->pfm", part_re, spectrum[:, :, 1]) + hsum(
        "fpr,frm->pfm", part_im, spectrum[:, :, 0]
    )
    mine = sum_at_owner(jnp.stack([real_out, imag_out], 2), "team", 0)
    received = lax.all_to_all(mine, "facet", split_axis=1, concat_axis=1, tiled=True)
    block_rows = received.shape[0]
    phase_cos, phase_sin = facet_phase(
        my_team * share + jnp.arange(block_rows, dtype=jnp.int32), facet_offsets
    )
    grid_re = jnp.sum(phase_cos * received[:, :, 0] - phase_sin * received[:, :, 1], 1) * norm
    grid_im = jnp.sum(phase_cos * received[:, :, 1] + phase_sin * received[:, :, 0], 1) * norm
    assembled = collect(jnp.stack([grid_re, grid_im], 1), "team", 0)
    maps = aterm[0].astype(jnp.float32)
    own_map = lax.dynamic_index_in_dim(maps, my_side, 0, keepdims=False)
    weighted = weigh_image(assembled, own_map, k_re, k_im)
    own_cells = cells[0, :, 0]
    own_obs = observed[0, :, 0]
    own_weights = weights[0, :, 0]
    zero_int = jnp.zeros((), jnp.int32)
    lane_ids = jnp.arange(VB, dtype=jnp.int32)
    empty_grid = jnp.zeros((SG, 2 * SG), jnp.float32)

    def block_term(side, block, image_stack):
        start = block * VB
        cell_pair = lax.dynamic_slice(own_cells, (side, zero_int, start), (1, 2, VB))[0]
        obs_pair = lax.dynamic_slice(own_obs, (side, zero_int, start), (1, 2, VB))[0].astype(
            jnp.float32
        )
        weight = lax.dynamic_slice(own_weights, (side, start), (1, VB))[0].astype(jnp.float32)
        live = (start + lane_ids < counts[my_facet, side, my_team]).astype(jnp.float32)
        return degrid_block(image_stack, cell_pair, obs_pair, weight, live)

    own_blocks = (counts[my_facet, my_side, my_team] + VB - 1) // VB

    def own_step(block, total):
        return total + block_term(my_side, block, weighted)

    grid = lax.fori_loop(0, own_blocks, own_step, empty_grid)
    returned = to_return(grid, own_map, k_re, k_im)
    total_back = over_copies(returned.astype(jnp.bfloat16), "team").astype(jnp.float32)
    block_rows = total_back.shape[0]
    phase_cos, phase_sin = facet_phase(jnp.arange(block_rows, dtype=jnp.int32), facet_offsets)
    back_re = (phase_cos * total_back[:, None, 0] + phase_sin * total_back[:, None, 1]) * norm
    back_im = (phase_cos * total_back[:, None, 1] - phase_sin * total_back[:, None, 0]) * norm
    arrived = lax.all_to_all(
        jnp.stack([back_re, back_im], 2).astype(jnp.bfloat16),
        "facet",
        split_axis=1,
        concat_axis=1,
        tiled=True,
    ).astype(jnp.float32)
    part_re = w_re
    part_im = w_im
    fold_re = hsum("fpr,pfm->frm", part_re, arrived[:, :, 0]) + hsum(
        "fpr,pfm->frm", part_im, arrived[:, :, 1]
    )
    fold_im = hsum("fpr,pfm->frm", part_re, arrived[:, :, 1]) - hsum(
        "fpr,pfm->frm", part_im, arrived[:, :, 0]
    )
    folded = jnp.stack([fold_re, fold_im], 2)
    folded_stack = folded.astype(jnp.bfloat16).reshape(n_facet * rows_dev, 2 * M)
    half = L // n_sub
    col_start = my_side * half
    other_stack = partner(folded_stack, "sub", 0)
    both_stacks = jnp.concatenate([folded_stack, other_stack], 0)
    back_half = jnp.concatenate(
        [
            lax.dynamic_slice_in_dim(backward, col_start, half, 1),
            lax.dynamic_slice_in_dim(backward, L + col_start, half, 1),
        ],
        1,
    )
    spectra_half = jnp.dot(both_stacks, back_half, preferred_element_type=jnp.float32).reshape(
        2 * n_facet, rows_dev, 2, half
    )
    other_ids = jnp.arange(n_facet, dtype=jnp.int32) * n_sub + (1 - my_side)
    all_tunings = jnp.concatenate([tunings, sub_offsets[other_ids, 1]], 0)
    half_cols = col_start + jnp.arange(half, dtype=jnp.int32)
    half_angle = angles(all_tunings[:, None], half_cols[None, :], L)
    half_cos = jnp.cos(half_angle)[:, None, :]
    half_sin = jnp.sin(half_angle)[:, None, :]
    update_re = jnp.sum(spectra_half[:, :, 0] * half_cos - spectra_half[:, :, 1] * half_sin, 0)
    update_im = jnp.sum(spectra_half[:, :, 1] * half_cos + spectra_half[:, :, 0] * half_sin, 0)
    return jnp.stack([update_re, update_im], 0)[None]


def solution(mesh):
    placed = (
        P("facet", None, "team", None),
        P(),
        P(),
        P("facet", None, None, None),
        P("facet", None, "team", None, None),
        P("facet", None, "team", None, None),
        P("facet", None, "team", None),
        P(),
    )
    return jax.shard_map(
        local,
        mesh=mesh,
        in_specs=placed,
        out_specs=P("facet", None, "team", "sub"),
        check_vma=False,
    )
```

profile of v0, /device:TPU:1, one launch (start us, length us, event | category | flops | bytes accessed | tf_op | source)
XLA Modules:
  0.0 229.4 jit_solution(1294391637697271506)
XLA Ops:
  0.0 8.5 %multiply_convert_fusion.2 = (bf16[4096,128]{0,1:T(8,128)(2,1)S(1)}, bf16[4096,128]{0,1:T(8,128)(2,1)S(1)}) fusion(), kind=kLoop, calls=%fused_computation.82 | loop fusion | flops 9961472 | bytes 2097152 | tf_op jit(solution)/shard_map/convert_element_type | solution.py:62
  8.5 7.9 %fusion.68 = bf16[4096,128]{0,1:T(8,128)(2,1)S(1)} fusion(), kind=kLoop, calls=%fused_computation.135 | loop fusion | flops 10485760 | bytes 1048576 | tf_op jit(solution)/shard_map/neg | solution.py:64
  17.7 1.9 fusion.126
  19.5 1.5 bitcast_convert_fusion.1
  21.1 1.2 gather_fusion
  23.0 18.1 %maximum_maximum_fusion = bf16[8192,256]{0,1:T(8,128)(2,1)S(1)} fusion(bf16[4096,128]{0,1:T(8,128)(2,1)S(1)} %get-tuple-element.313, bf16[4096,128]{0,1:T(8,128)(2,1)S(1)} %fusion.68, bf16[4096,128]{0,1:T(8,128)(2,1)S(1)} %get-tuple-element.312), kind=kLoop, calls=%fused_computation.51 | loop fusion | flops 16777216 | bytes 7340032 | tf_op jit(solution)/shard_map/concatenate | solution.py:63
  41.6 1.5 fusion.36
  43.1 1.9 fusion.141
  45.0 1.9 fusion.142
  47.0 1.9 convolution_subtract_fusion
  48.9 1.9 convolution_add_fusion.1
  51.1 1.5 copy.42
  52.6 9.1 %all-to-all-start = ((f32[8,16,16,2,128]{4,1,2,3,0:T(8,128)}), f32[8,16,16,2,128]{4,1,2,3,0:T(8,128)S(1)}, u32[]{:S(2)}, u32[]{:S(2)}) async-start(f32[8,16,16,2,128]{4,1,2,3,0:T(8,128)} %copy.42), calls=%async_computation | async-start | bytes 4194304 | tf_op jit(solution)/shard_map/all_to_all | solution.py:22
  62.8 7.9 %fusion.69 = bf16[128,4096]{1,0:T(8,128)(2,1)S(1)} fusion(), kind=kLoop, calls=%fused_computation.136 | loop fusion | flops 9961472 | bytes 1048576 | tf_op jit(solution)/shard_map/neg | solution.py:69
  70.7 39.6 %all-to-all-done = f32[8,16,16,2,128]{4,1,2,3,0:T(8,128)S(1)} async-done(((f32[8,16,16,2,128]{4,1,2,3,0:T(8,128)}), f32[8,16,16,2,128]{4,1,2,3,0:T(8,128)S(1)}, u32[]{:S(2)}, u32[]{:S(2)}) %all-to-all-start) | async-done | bytes 2097184 | tf_op jit(solution)/shard_map/all_to_all | solution.py:22
  111.1 9.4 %all-to-all-start.1 = ((f32[16,16,2,128]{3,0,2,1:T(8,128)}), f32[16,16,2,128]{3,0,2,1:T(8,128)S(1)}, u32[]{:S(2)}, u32[]{:S(2)}) async-start(f32[16,16,2,128]{3,0,2,1:T(8,128)} %copy.34), calls=%async_computation.1 | async-start | bytes 524288 | tf_op jit(solution)/shard_map/all_to_all | solution.py:207
  120.6 1.3 dynamic_slice.40
  122.6 5.0 %all-to-all-done.1 = f32[16,16,2,128]{3,0,2,1:T(8,128)S(1)} async-done(((f32[16,16,2,128]{3,0,2,1:T(8,128)}), f32[16,16,2,128]{3,0,2,1:T(8,128)S(1)}, u32[]{:S(2)}, u32[]{:S(2)}) %all-to-all-start.1) | async-done | bytes 262176 | tf_op jit(solution)/shard_map/all_to_all | solution.py:207
  129.0 3.5 %all-to-all-start.2 = ((f32[8,16,2,128]{3,2,1,0:T(2,128)}), f32[8,16,2,128]{3,2,1,0:T(2,128)S(1)}, u32[]{:S(2)}, u32[]{:S(2)}) async-start(f32[8,16,2,128]{3,2,1,0:T(2,128)} %broadcast_in_dim.9), calls=%async_computation.2 | async-start | bytes 262144 | tf_op jit(solution)/shard_map/all_to_all | solution.py:34
  132.5 1.1 cosine_convert_fusion.2
  133.6 6.5 %all-to-all-done.2 = f32[8,16,2,128]{3,2,1,0:T(2,128)S(1)} async-done(((f32[8,16,2,128]{3,2,1,0:T(2,128)}), f32[8,16,2,128]{3,2,1,0:T(2,128)S(1)}, u32[]{:S(2)}, u32[]{:S(2)}) %all-to-all-start.2) | async-done | bytes 131104 | tf_op jit(solution)/shard_map/all_to_all | solution.py:34
  142.0 0.8 convolution_subtract_fusion.3
  142.8 0.9 fusion.138
  143.7 0.9 fusion.140
  145.4 0.9 fusion.51
  146.3 0.9 fusion.52
  147.5 1.2 fusion.73
  148.7 5.3 %while.15 = (s32[]{:T(128)}, f32[256,512]{1,0:T(8,128)S(1)}, s32[]{:T(128)}, s32[1,2,256]{2,1,0:T(2,128)S(1)}, s32[1,1,1]{2,1,0:T(1,128)}, /*index=5*/bf16[1,256...) while((s32[]{:T(128)}, f32[256,512]{1,0:T(8,128)S(1)}, ...), condition=%wide.region_6.7_spmd.clone, body=%wide.region_5.6_spmd.clone.sunk | while | flops 141363712 | bytes 2383489 | solution.py:240
  149.4 1.3 fusion.327
  150.7 1.3 fusion.328
  152.0 1.3 cosine_convert_fusion.5
  160.5 0.9 broadcast_in_dim.10
  161.4 4.1 %all-to-all-start.3 = ((bf16[8,128,2,128]{3,1,2,0:T(8,128)(2,1)}), bf16[8,128,2,128]{3,1,2,0:T(8,128)(2,1)}, u32[]{:S(2)}, u32[]{:S(2)}) async-start(bf16[8,128,2,128]{3,1,2,0:T(8,128)(2,1)} %broadcast_in_dim.10), calls=%async_computation.3 | async-start | bytes 1048576 | tf_op jit(solution)/shard_map/all_to_all | solution.py:34
  165.5 1.9 fusion.120
  167.4 8.5 %multiply_convert_fusion = (bf16[128,4096]{1,0:T(8,128)(2,1)S(1)}, bf16[128,4096]{1,0:T(8,128)(2,1)S(1)}) fusion(), kind=kLoop, calls=%fused_computation.78 | loop fusion | flops 9437184 | bytes 2097152 | tf_op jit(solution)/shard_map/convert_element_type | solution.py:67
  175.9 4.8 %all-to-all-done.3 = bf16[8,128,2,128]{3,1,2,0:T(8,128)(2,1)} async-done(((bf16[8,128,2,128]{3,1,2,0:T(8,128)(2,1)}), bf16[8,128,2,128]{3,1,2,0:T(8,128)(2,1)}, u32[]{:S(2)}, u32[]{:S(2)}) %all-to-all-start.3) | async-done | bytes 524320 | tf_op jit(solution)/shard_map/all_to_all | solution.py:34
  180.7 1.1 convert_reduce_fusion
  181.8 4.8 %multiply_convert_fusion.5 = (bf16[128,16,1,128]{3,0,2,1:T(8,128)(2,1)S(1)}, bf16[128,16,1,128]{3,0,2,1:T(8,128)(2,1)S(1)}) fusion(f32[128,128]{1,0:T(8,128)S(1)} %get-tuple-element.295, f32[128,128]{1,0:T(8,128)S(1)} %get-tuple-element.294, s32[16,128]{1,0:T(8,128)S(1)} %add_select_fusion.15, s32[128,16]{0,1:T(8,128)S(1)} %add_select_fusion.16), kind=kLoop, calls=%fused_computation.124 | loop fusion | flops 6291456 | bytes 1196032 | tf_op jit(solution)/shard_map/convert.7
  186.7 1.1 pad_maximum_fusion.1
  187.7 8.2 %all-to-all-start.4 = ((bf16[128,16,2,128]{3,0,2,1:T(8,128)(2,1)}), bf16[128,16,2,128]{3,0,2,1:T(8,128)(2,1)}, u32[]{:S(2)}, u32[]{:S(2)}) async-start(bf16[128,16,2,128]{3,0,2,1:T(8,128)(2,1)} %pad_maximum_fusion.1), calls=%async_computation.4 | async-start | bytes 2097152 | tf_op jit(solution)/shard_map/all_to_all | solution.py:247
  196.0 18.6 %maximum_maximum_fusion.1 = bf16[256,8192]{1,0:T(8,128)(2,1)} fusion(bf16[128,4096]{1,0:T(8,128)(2,1)S(1)} %get-tuple-element.315, bf16[128,4096]{1,0:T(8,128)(2,1)S(1)} %fusion.69, bf16[128,4096]{1,0:T(8,128)(2,1)S(1)} %get-tuple-element.314), kind=kLoop, calls=%fused_computation.52 | loop fusion | flops 16777216 | bytes 7340032 | tf_op jit(solution)/shard_map/concatenate | solution.py:68
  214.5 1.8 fusion.66
  216.3 1.8 fusion.67
  218.1 1.8 fusion.60
  219.9 1.8 fusion.59
  221.6 2.5 %collective-permute-start = (bf16[128,256]{1,0:T(8,128)(2,1)S(1)}, bf16[128,256]{1,0:T(8,128)(2,1)S(1)}, u32[]{:S(2)}, u32[]{:S(2)}) collective-permute-start(bf16[128,256]{1,0:T(8,128)(2,1)S(1)} %copy_bitcast_fusion), channel_id=1, source_target_pairs={{0,1},{1,0},{2,3},{3,2},{4,5},{5,4},{6,7},{7,6},{8,9},{9,8},{10,11... | collective-permute-start | bytes 196616 | tf_op jit(solution)/shard_map/ppermute | solution.py:48
  224.2 1.7 constant_dynamic-slice_fusion.1
  225.9 1.1 collective-permute-done
  (79 shorter events, 18.6 us)
Async XLA Ops:
  0.0 62.5 %copy-start = (s32[1,2,1,2,256]{4,3,2,1,0:T(2,128)S(1)}, s32[1,2,1,2,256]{4,3,2,1,0:T(2,128)}, u32[]{:S(2)}) copy-start(s32[1,2,1,2,256]{4,3,2,1,0:T(2,128)} %param.14) | copy-start | bytes 12292
  0.0 16.4 %copy-start.1 = (s32[32,2]{0,1:T(2,128)S(1)}, s32[32,2]{0,1:T(2,128)}, u32[]{:S(2)}) copy-start(s32[32,2]{0,1:T(2,128)} %param.11) | copy-start | bytes 772
  17.1 0.6 copy-start.7
  23.0 25.9 %copy-start.5 = (s32[8]{0:T(128)}, s32[8]{0:T(128)S(1)}, u32[]{:S(2)}) copy-start(s32[8]{0:T(128)S(1)} %iota_add_fusion.4) | copy-start | bytes 100
  23.0 18.1 %copy-start.3 = (f32[16,4096]{1,0:T(8,128)S(1)}, f32[16,4096]{1,0:T(8,128)}, u32[]{:S(2)}) copy-start(f32[16,4096]{1,0:T(8,128)} %get-tuple-element.309) | copy-start | bytes 786436
  23.0 18.1 %copy-start.4 = (f32[8,4096]{1,0:T(8,128)S(1)}, f32[8,4096]{1,0:T(8,128)}, u32[]{:S(2)}) copy-start(f32[8,4096]{1,0:T(8,128)} %get-tuple-element.299) | copy-start | bytes 393220
  52.6 9.9 %copy-start.9 = (bf16[1,2,1,256]{3,1,2,0:T(2,128)(2,1)S(1)}, bf16[1,2,1,256]{3,1,2,0:T(2,128)(2,1)}, u32[]{:S(2)}) copy-start(bf16[1,2,1,256]{3,1,2,0:T(2,128)(2,1)} %param.16) | copy-start | bytes 3076
  52.6 9.9 %copy-start.11 = (bf16[1,2,1,2,256]{4,3,2,1,0:T(2,128)(2,1)S(1)}, bf16[1,2,1,2,256]{4,3,2,1,0:T(2,128)(2,1)}, u32[]{:S(2)}) copy-start(bf16[1,2,1,2,256]{4,3,2,1,0:T(2,128)(2,1)} %param.15) | copy-start | bytes 6148
  52.6 9.9 %copy-start.10 = (s32[16,2]{0,1:T(2,128)S(1)}, s32[16,2]{0,1:T(2,128)}, u32[]{:S(2)}) copy-start(s32[16,2]{0,1:T(2,128)} %param.12) | copy-start | bytes 388
  52.6 57.6 %all-to-all-start = ((f32[8,16,16,2,128]{4,1,2,3,0:T(8,128)}), f32[8,16,16,2,128]{4,1,2,3,0:T(8,128)S(1)}, u32[]{:S(2)}, u32[]{:S(2)}) async-start(f32[8,16,16,2,128]{4,1,2,3,0:T(8,128)} %copy.42), calls=%async_computation | async-start | bytes 4194304 | tf_op jit(solution)/shard_map/all_to_all | solution.py:22
  62.8 57.8 %copy-start.8 = (s32[16]{0:T(128)S(1)}, s32[16]{0:T(128)}, u32[]{:S(2)}) copy-start(s32[16]{0:T(128)} %copy-done.7) | copy-start | bytes 196
  111.1 16.5 %all-to-all-start.1 = ((f32[16,16,2,128]{3,0,2,1:T(8,128)}), f32[16,16,2,128]{3,0,2,1:T(8,128)S(1)}, u32[]{:S(2)}, u32[]{:S(2)}) async-start(f32[16,16,2,128]{3,0,2,1:T(8,128)} %copy.34), calls=%async_computation.1 | async-start | bytes 524288 | tf_op jit(solution)/shard_map/all_to_all | solution.py:207
  129.0 16.5 %copy-start.12 = (bf16[1,2,256,256]{3,2,1,0:T(8,128)(2,1)S(1)}, bf16[1,2,256,256]{3,2,1,0:T(8,128)(2,1)}, u32[]{:S(2)}) copy-start(bf16[1,2,256,256]{3,2,1,0:T(8,128)(2,1)} %param.13) | copy-start | bytes 786436
  129.0 11.2 %all-to-all-start.2 = ((f32[8,16,2,128]{3,2,1,0:T(2,128)}), f32[8,16,2,128]{3,2,1,0:T(2,128)S(1)}, u32[]{:S(2)}, u32[]{:S(2)}) async-start(f32[8,16,2,128]{3,2,1,0:T(2,128)} %broadcast_in_dim.9), calls=%async_computation.2 | async-start | bytes 262144 | tf_op jit(solution)/shard_map/all_to_all | solution.py:34
  161.4 19.3 %all-to-all-start.3 = ((bf16[8,128,2,128]{3,1,2,0:T(8,128)(2,1)}), bf16[8,128,2,128]{3,1,2,0:T(8,128)(2,1)}, u32[]{:S(2)}, u32[]{:S(2)}) async-start(bf16[8,128,2,128]{3,1,2,0:T(8,128)(2,1)} %broadcast_in_dim.10), calls=%async_computation.3 | async-start | bytes 1048576 | tf_op jit(solution)/shard_map/all_to_all | solution.py:34
  187.7 26.8 %all-to-all-start.4 = ((bf16[128,16,2,128]{3,0,2,1:T(8,128)(2,1)}), bf16[128,16,2,128]{3,0,2,1:T(8,128)(2,1)}, u32[]{:S(2)}, u32[]{:S(2)}) async-start(bf16[128,16,2,128]{3,0,2,1:T(8,128)(2,1)} %pad_maximum_fusion.1), calls=%async_computation.4 | async-start | bytes 2097152 | tf_op jit(solution)/shard_map/all_to_all | solution.py:247
  195.9 18.6 %copy-start.6 = (s32[8]{0:T(128)S(1)}, s32[8]{0:T(128)}, u32[]{:S(2)}) copy-start(s32[8]{0:T(128)} %copy-done.5) | copy-start | bytes 100
  221.6 5.3 %collective-permute-start = (bf16[128,256]{1,0:T(8,128)(2,1)S(1)}, bf16[128,256]{1,0:T(8,128)(2,1)S(1)}, u32[]{:S(2)}, u32[]{:S(2)}) collective-permute-start(bf16[128,256]{1,0:T(8,128)(2,1)S(1)} %copy_bitcast_fusion), channel_id=1, source_target_pairs={{0,1},{1,0},{2,3},{3,2},{4,5},{5,4},{6,7},{7,6},{8,9},{9,8},{10,11... | collective-permute-start | bytes 196616 | tf_op jit(solution)/shard_map/ppermute | solution.py:48
  227.0 1.0 copy-start.2
where the time goes:
time: 233 us; the launch traced here: 229 us
  other arithmetic  92.4 us (40%)
  waiting for transfers between devices  57 us (24%)
  starting transfers between devices  37 us (16%)
  matrix products  30.9 us (13%)
  local copies, waits for them, and re-layouts  10.5 us (5%)
    all_to_all x1, waiting for transfers between devices, sum_at_owner(): parts = lax.all_to_all(cut_along(shard, dim, peers), axis, 0, 0, tiled=True)  39.6 us
    concatenate x1, other arithmetic, transform_tables(): jnp.concatenate([jnp.concatenate([back_re, back_im], 1), jnp.concatenate(...  18.6 us
    concatenate x1, other arithmetic, transform_tables(): jnp.concatenate([jnp.concatenate([spec_re, spec_im], 1), jnp.concatenate(...  18.1 us
    dot_general x8, matrix products, hsum(): jnp.einsum(form, left, right, precision=HIGHEST, preferred_element_type=j...  14.8 us
    dot_general x16, matrix products, hdot(): jnp.dot(left, right, precision=HIGHEST, preferred_element_type=jnp.float32)  13.2 us
    all_to_all x2, waiting for transfers between devices, from_everyone(): return lax.all_to_all(copies, axis, split_axis=0, concat_axis=0, tiled=True)  11.3 us
    all_to_all x1, starting transfers between devices, local(): lax.all_to_all(mine, 'facet', split_axis=1, concat_axis=1, tiled=True)  9.44 us
    all_to_all x1, starting transfers between devices, sum_at_owner(): parts = lax.all_to_all(cut_along(shard, dim, peers), axis, 0, 0, tiled=True)  9.15 us
  transfers between devices with their start and end apart: 6, of which 5 were waited for; matrix products, arithmetic and copies ran while one was open for 18% of the time, Pallas kernels for 0%

commit v1 on v0

--- a/solution.py
+++ b/solution.py
@@ -3,6 +3,7 @@
 import jax.numpy as jnp
 from jax import lax
 from jax.sharding import PartitionSpec as P
+from jax.lax import all_to_all, psum
 
 L = 4096
 M = 128
@@ -244,12 +245,18 @@
     phase_cos, phase_sin = facet_phase(jnp.arange(block_rows, dtype=jnp.int32), facet_offsets)
     back_re = (phase_cos * total_back[:, None, 0] + phase_sin * total_back[:, None, 1]) * norm
     back_im = (phase_cos * total_back[:, None, 1] - phase_sin * total_back[:, None, 0]) * norm
-    arrived = lax.all_to_all(
-        jnp.stack([back_re, back_im], 2).astype(jnp.bfloat16),
-        "facet",
-        split_axis=1,
-        concat_axis=1,
-        tiled=True,
+    arrived = jnp.concatenate(
+        all_to_all(
+            jnp.stack(
+                jnp.split(
+                    jnp.stack([back_re, back_im], 2).astype(jnp.bfloat16), psum(1, "facet"), axis=1
+                )
+            ),
+            "facet",
+            0,
+            0,
+        ),
+        axis=1,
     ).astype(jnp.float32)
     part_re = w_re
     part_im = w_im

time: 233 us -> 239 us (1.026)
  other arithmetic: 92.4 us -> 101 us
  matrix products: 30.9 us -> 26.7 us
    unnamed x0 -> x15, other arithmetic: none -> 9.48 us
    dot_general x8, matrix products: 14.8 us -> 10.6 us  [hsum(): jnp.einsum(form, left, right, precision=HIGHEST, preferred_element_type=j...]
  transfers between devices with their start and end apart: 6 -> 6, of which waited for: 5 -> 5; matrix products, arithmetic and copies ran while one was open for 18% -> 17% of each run, Pallas kernels for 0% -> 0%
where the time goes in v1:
time: 239 us; the launch traced here: 236 us
  other arithmetic  101 us (42%)
  waiting for transfers between devices  58.4 us (24%)
  starting transfers between devices  36.9 us (15%)
  matrix products  26.7 us (11%)
  local copies, waits for them, and re-layouts  10.6 us (4%)
    all_to_all x1, waiting for transfers between devices, sum_at_owner(): parts = lax.all_to_all(cut_along(shard, dim, peers), axis, 0, 0, tiled=True)  39.6 us
    concatenate x1, other arithmetic, transform_tables(): jnp.concatenate([jnp.concatenate([back_re, back_im], 1), jnp.concatenate(...  18.6 us
    concatenate x1, other arithmetic, transform_tables(): jnp.concatenate([jnp.concatenate([spec_re, spec_im], 1), jnp.concatenate(...  18.1 us
    dot_general x16, matrix products, hdot(): jnp.dot(left, right, precision=HIGHEST, preferred_element_type=jnp.float32)  13.2 us
    all_to_all x2, waiting for transfers between devices, from_everyone(): return lax.all_to_all(copies, axis, split_axis=0, concat_axis=0, tiled=True)  11.3 us
    dot_general x8, matrix products, hsum(): jnp.einsum(form, left, right, precision=HIGHEST, preferred_element_type=j...  10.6 us
    unnamed x15, other arithmetic  9.48 us
    all_to_all x1, starting transfers between devices, local(): lax.all_to_all(mine, 'facet', split_axis=1, concat_axis=1, tiled=True)  9.44 us
  transfers between devices with their start and end apart: 6, of which 5 were waited for; matrix products, arithmetic and copies ran while one was open for 17% of the time, Pallas kernels for 0%

profile of v1, /device:TPU:1, one launch (start us, length us, event | category | flops | bytes accessed | tf_op | source)
XLA Modules:
  0.0 235.9 jit_solution(14208395100464343898)
XLA Ops:
  0.0 8.5 %multiply_convert_fusion.2 = (bf16[4096,128]{0,1:T(8,128)(2,1)S(1)}, bf16[4096,128]{0,1:T(8,128)(2,1)S(1)}) fusion(), kind=kLoop, calls=%fused_computation.112 | loop fusion | flops 9961472 | bytes 2097152 | tf_op jit(solution)/shard_map/convert_element_type | solution.py:63
  8.5 7.9 %fusion.68 = bf16[4096,128]{0,1:T(8,128)(2,1)S(1)} fusion(), kind=kLoop, calls=%fused_computation.165 | loop fusion | flops 10485760 | bytes 1048576 | tf_op jit(solution)/shard_map/neg | solution.py:65
  17.7 1.9 fusion.126
  19.6 1.5 bitcast_convert_fusion.1
  21.1 1.2 gather_fusion
  23.1 18.1 %maximum_maximum_fusion = bf16[8192,256]{0,1:T(8,128)(2,1)S(1)} fusion(bf16[4096,128]{0,1:T(8,128)(2,1)S(1)} %get-tuple-element.313, bf16[4096,128]{0,1:T(8,128)(2,1)S(1)} %fusion.68, bf16[4096,128]{0,1:T(8,128)(2,1)S(1)} %get-tuple-element.312), kind=kLoop, calls=%fused_computation.51 | loop fusion | flops 16777216 | bytes 7340032 | tf_op jit(solution)/shard_map/concatenate | solution.py:64
  41.7 1.5 fusion.36
  43.2 1.9 fusion.158
  45.2 1.9 fusion.159
  47.1 1.9 convolution_subtract_fusion
  49.0 1.9 convolution_add_fusion.1
  51.2 1.5 copy.70
  52.8 9.1 %all-to-all-start = ((f32[8,16,16,2,128]{4,1,2,3,0:T(8,128)}), f32[8,16,16,2,128]{4,1,2,3,0:T(8,128)S(1)}, u32[]{:S(2)}, u32[]{:S(2)}) async-start(f32[8,16,16,2,128]{4,1,2,3,0:T(8,128)} %copy.70), calls=%async_computation | async-start | bytes 4194304 | tf_op jit(solution)/shard_map/all_to_all | solution.py:23
  62.9 7.9 %fusion.69 = bf16[128,4096]{1,0:T(8,128)(2,1)S(1)} fusion(), kind=kLoop, calls=%fused_computation.166 | loop fusion | flops 9961472 | bytes 1048576 | tf_op jit(solution)/shard_map/neg | solution.py:70
  70.8 39.6 %all-to-all-done = f32[8,16,16,2,128]{4,1,2,3,0:T(8,128)S(1)} async-done(((f32[8,16,16,2,128]{4,1,2,3,0:T(8,128)}), f32[8,16,16,2,128]{4,1,2,3,0:T(8,128)S(1)}, u32[]{:S(2)}, u32[]{:S(2)}) %all-to-all-start) | async-done | bytes 2097184 | tf_op jit(solution)/shard_map/all_to_all | solution.py:23
  111.2 9.4 %all-to-all-start.1 = ((f32[16,16,2,128]{3,0,2,1:T(8,128)}), f32[16,16,2,128]{3,0,2,1:T(8,128)S(1)}, u32[]{:S(2)}, u32[]{:S(2)}) async-start(f32[16,16,2,128]{3,0,2,1:T(8,128)} %copy.63), calls=%async_computation.1 | async-start | bytes 524288 | tf_op jit(solution)/shard_map/all_to_all | solution.py:208
  120.8 1.3 dynamic_slice.40
  122.8 4.9 %all-to-all-done.1 = f32[16,16,2,128]{3,0,2,1:T(8,128)S(1)} async-done(((f32[16,16,2,128]{3,0,2,1:T(8,128)}), f32[16,16,2,128]{3,0,2,1:T(8,128)S(1)}, u32[]{:S(2)}, u32[]{:S(2)}) %all-to-all-start.1) | async-done | bytes 262176 | tf_op jit(solution)/shard_map/all_to_all | solution.py:208
  129.1 3.5 %all-to-all-start.2 = ((f32[8,16,2,128]{3,2,1,0:T(2,128)}), f32[8,16,2,128]{3,2,1,0:T(2,128)S(1)}, u32[]{:S(2)}, u32[]{:S(2)}) async-start(f32[8,16,2,128]{3,2,1,0:T(2,128)} %broadcast_in_dim.9), calls=%async_computation.2 | async-start | bytes 262144 | tf_op jit(solution)/shard_map/all_to_all | solution.py:35
  132.6 1.1 cosine_convert_fusion.2
  133.7 6.5 %all-to-all-done.2 = f32[8,16,2,128]{3,2,1,0:T(2,128)S(1)} async-done(((f32[8,16,2,128]{3,2,1,0:T(2,128)}), f32[8,16,2,128]{3,2,1,0:T(2,128)S(1)}, u32[]{:S(2)}, u32[]{:S(2)}) %all-to-all-start.2) | async-done | bytes 131104 | tf_op jit(solution)/shard_map/all_to_all | solution.py:35
  140.4 0.8 fusion.154
  141.3 0.8 fusion.156
  142.1 0.8 convolution_subtract_fusion.3
  143.0 0.9 fusion.155
  143.8 0.9 fusion.157
  144.7 0.8 convolution_add_fusion.4
  145.6 0.9 fusion.51
  146.5 0.9 fusion.52
  147.6 1.2 fusion.73
  148.9 5.3 %while.15 = (s32[]{:T(128)}, f32[256,512]{1,0:T(8,128)S(1)}, s32[]{:T(128)}, s32[1,2,256]{2,1,0:T(2,128)S(1)}, s32[1,1,1]{2,1,0:T(1,128)}, /*index=5*/bf16[1,256...) while((s32[]{:T(128)}, f32[256,512]{1,0:T(8,128)S(1)}, ...), condition=%wide.region_6.7_spmd.clone, body=%wide.region_5.6_spmd.clone.sunk | while | flops 141363712 | bytes 2383489 | solution.py:241
  149.6 1.3 fusion.344
  150.9 1.3 fusion.345
  152.2 1.3 cosine_convert_fusion.5
  155.9 0.8 convolution_add_fusion.3
  157.5 0.8 convolution_subtract_fusion.2
  160.6 0.9 broadcast_in_dim.10
  161.6 4.1 %all-to-all-start.3 = ((bf16[8,128,2,128]{3,1,2,0:T(8,128)(2,1)}), bf16[8,128,2,128]{3,1,2,0:T(8,128)(2,1)}, u32[]{:S(2)}, u32[]{:S(2)}) async-start(bf16[8,128,2,128]{3,1,2,0:T(8,128)(2,1)} %broadcast_in_dim.10), calls=%async_computation.3 | async-start | bytes 1048576 | tf_op jit(solution)/shard_map/all_to_all | solution.py:35
  165.7 1.9 fusion.120
  167.6 8.5 %multiply_convert_fusion = (bf16[128,4096]{1,0:T(8,128)(2,1)S(1)}, bf16[128,4096]{1,0:T(8,128)(2,1)S(1)}) fusion(), kind=kLoop, calls=%fused_computation.108 | loop fusion | flops 9437184 | bytes 2097152 | tf_op jit(solution)/shard_map/convert_element_type | solution.py:68
  176.1 4.8 %all-to-all-done.3 = bf16[8,128,2,128]{3,1,2,0:T(8,128)(2,1)} async-done(((bf16[8,128,2,128]{3,1,2,0:T(8,128)(2,1)}), bf16[8,128,2,128]{3,1,2,0:T(8,128)(2,1)}, u32[]{:S(2)}, u32[]{:S(2)}) %all-to-all-start.3) | async-done | bytes 524320 | tf_op jit(solution)/shard_map/all_to_all | solution.py:35
  180.9 1.1 convert_reduce_fusion
  182.1 4.8 %multiply_convert_fusion.5 = (bf16[128,16,1,128]{3,0,2,1:T(8,128)(2,1)S(1)}, bf16[128,16,1,128]{3,0,2,1:T(8,128)(2,1)S(1)}) fusion(f32[128,128]{1,0:T(8,128)S(1)} %get-tuple-element.295, f32[128,128]{1,0:T(8,128)S(1)} %get-tuple-element.294, s32[16,128]{1,0:T(8,128)S(1)} %add_select_fusion.15, s32[128,16]{0,1:T(8,128)S(1)} %add_select_fusion.16), kind=kLoop, calls=%fused_computation.154 | loop fusion | flops 6291456 | bytes 1196032 | tf_op jit(solution)/shard_map/convert.7
  197.0 8.2 %all-to-all-start.4 = ((bf16[16,128,1,2,128]{4,1,3,2,0:T(8,128)(2,1)}), bf16[16,128,1,2,128]{4,1,3,2,0:T(8,128)(2,1)}, u32[]{:S(2)}, u32[]{:S(2)}) async-start(bf16[16,128,1,2,128]{4,1,3,2,0:T(8,128)(2,1)} %fusion.149), calls=%async_computation.4 | async-start | bytes 2097152 | tf_op jit(solution)/shard_map/all_to_all | solution.py:249
  205.2 18.6 %maximum_maximum_fusion.1 = bf16[256,8192]{1,0:T(8,128)(2,1)} fusion(bf16[128,4096]{1,0:T(8,128)(2,1)S(1)} %get-tuple-element.315, bf16[128,4096]{1,0:T(8,128)(2,1)S(1)} %fusion.69, bf16[128,4096]{1,0:T(8,128)(2,1)S(1)} %get-tuple-element.314), kind=kLoop, calls=%fused_computation.52 | loop fusion | flops 16777216 | bytes 7340032 | tf_op jit(solution)/shard_map/concatenate | solution.py:69
  223.8 1.4 copy.77
  228.2 2.5 %collective-permute-start = (bf16[128,256]{1,0:T(8,128)(2,1)S(1)}, bf16[128,256]{1,0:T(8,128)(2,1)S(1)}, u32[]{:S(2)}, u32[]{:S(2)}) collective-permute-start(bf16[128,256]{1,0:T(8,128)(2,1)S(1)} %copy_bitcast_fusion.1), channel_id=1, source_target_pairs={{0,1},{1,0},{2,3},{3,2},{4,5},{5,4},{6,7},{7,6},{8,9},{9,8},{10,11... | collective-permute-start | bytes 196616 | tf_op jit(solution)/shard_map/ppermute | solution.py:49
  230.9 2.5 %collective-permute-done = bf16[128,256]{1,0:T(8,128)(2,1)S(1)} collective-permute-done((bf16[128,256]{1,0:T(8,128)(2,1)S(1)}, bf16[128,256]{1,0:T(8,128)(2,1)S(1)}, u32[]{:S(2)}, u32[]{:S(2)}) %collective-permute-start) | collective-permute-done | bytes 65568 | tf_op jit(solution)/shard_map/ppermute | solution.py:49
  (97 shorter events, 27.8 us)
Async XLA Ops:
  0.0 62.7 %copy-start = (s32[1,2,1,2,256]{4,3,2,1,0:T(2,128)S(1)}, s32[1,2,1,2,256]{4,3,2,1,0:T(2,128)}, u32[]{:S(2)}) copy-start(s32[1,2,1,2,256]{4,3,2,1,0:T(2,128)} %param.14) | copy-start | bytes 12292
  0.0 16.4 %copy-start.1 = (s32[32,2]{0,1:T(2,128)S(1)}, s32[32,2]{0,1:T(2,128)}, u32[]{:S(2)}) copy-start(s32[32,2]{0,1:T(2,128)} %param.11) | copy-start | bytes 772
  17.1 0.6 copy-start.8
  23.1 25.9 %copy-start.6 = (s32[8]{0:T(128)}, s32[8]{0:T(128)S(1)}, u32[]{:S(2)}) copy-start(s32[8]{0:T(128)S(1)} %iota_add_fusion.4) | copy-start | bytes 100
  23.1 18.1 %copy-start.4 = (f32[16,4096]{1,0:T(8,128)S(1)}, f32[16,4096]{1,0:T(8,128)}, u32[]{:S(2)}) copy-start(f32[16,4096]{1,0:T(8,128)} %get-tuple-element.309) | copy-start | bytes 786436
  23.1 18.1 %copy-start.5 = (f32[8,4096]{1,0:T(8,128)S(1)}, f32[8,4096]{1,0:T(8,128)}, u32[]{:S(2)}) copy-start(f32[8,4096]{1,0:T(8,128)} %get-tuple-element.299) | copy-start | bytes 393220
  52.7 9.9 %copy-start.10 = (bf16[1,2,1,256]{3,1,2,0:T(2,128)(2,1)S(1)}, bf16[1,2,1,256]{3,1,2,0:T(2,128)(2,1)}, u32[]{:S(2)}) copy-start(bf16[1,2,1,256]{3,1,2,0:T(2,128)(2,1)} %param.16) | copy-start | bytes 3076
  52.7 9.9 %copy-start.12 = (bf16[1,2,1,2,256]{4,3,2,1,0:T(2,128)(2,1)S(1)}, bf16[1,2,1,2,256]{4,3,2,1,0:T(2,128)(2,1)}, u32[]{:S(2)}) copy-start(bf16[1,2,1,2,256]{4,3,2,1,0:T(2,128)(2,1)} %param.15) | copy-start | bytes 6148
  52.8 9.9 %copy-start.11 = (s32[16,2]{0,1:T(2,128)S(1)}, s32[16,2]{0,1:T(2,128)}, u32[]{:S(2)}) copy-start(s32[16,2]{0,1:T(2,128)} %param.12) | copy-start | bytes 388
  52.8 57.6 %all-to-all-start = ((f32[8,16,16,2,128]{4,1,2,3,0:T(8,128)}), f32[8,16,16,2,128]{4,1,2,3,0:T(8,128)S(1)}, u32[]{:S(2)}, u32[]{:S(2)}) async-start(f32[8,16,16,2,128]{4,1,2,3,0:T(8,128)} %copy.70), calls=%async_computation | async-start | bytes 4194304 | tf_op jit(solution)/shard_map/all_to_all | solution.py:23
  62.9 57.8 %copy-start.9 = (s32[16]{0:T(128)S(1)}, s32[16]{0:T(128)}, u32[]{:S(2)}) copy-start(s32[16]{0:T(128)} %copy-done.8) | copy-start | bytes 196
  111.2 16.5 %all-to-all-start.1 = ((f32[16,16,2,128]{3,0,2,1:T(8,128)}), f32[16,16,2,128]{3,0,2,1:T(8,128)S(1)}, u32[]{:S(2)}, u32[]{:S(2)}) async-start(f32[16,16,2,128]{3,0,2,1:T(8,128)} %copy.63), calls=%async_computation.1 | async-start | bytes 524288 | tf_op jit(solution)/shard_map/all_to_all | solution.py:208
  129.1 16.5 %copy-start.13 = (bf16[1,2,256,256]{3,2,1,0:T(8,128)(2,1)S(1)}, bf16[1,2,256,256]{3,2,1,0:T(8,128)(2,1)}, u32[]{:S(2)}) copy-start(bf16[1,2,256,256]{3,2,1,0:T(8,128)(2,1)} %param.13) | copy-start | bytes 786436
  129.1 11.2 %all-to-all-start.2 = ((f32[8,16,2,128]{3,2,1,0:T(2,128)}), f32[8,16,2,128]{3,2,1,0:T(2,128)S(1)}, u32[]{:S(2)}, u32[]{:S(2)}) async-start(f32[8,16,2,128]{3,2,1,0:T(2,128)} %broadcast_in_dim.9), calls=%async_computation.2 | async-start | bytes 262144 | tf_op jit(solution)/shard_map/all_to_all | solution.py:35
  161.6 19.4 %all-to-all-start.3 = ((bf16[8,128,2,128]{3,1,2,0:T(8,128)(2,1)}), bf16[8,128,2,128]{3,1,2,0:T(8,128)(2,1)}, u32[]{:S(2)}, u32[]{:S(2)}) async-start(bf16[8,128,2,128]{3,1,2,0:T(8,128)(2,1)} %broadcast_in_dim.10), calls=%async_computation.3 | async-start | bytes 1048576 | tf_op jit(solution)/shard_map/all_to_all | solution.py:35
  197.0 26.8 %all-to-all-start.4 = ((bf16[16,128,1,2,128]{4,1,3,2,0:T(8,128)(2,1)}), bf16[16,128,1,2,128]{4,1,3,2,0:T(8,128)(2,1)}, u32[]{:S(2)}, u32[]{:S(2)}) async-start(bf16[16,128,1,2,128]{4,1,3,2,0:T(8,128)(2,1)} %fusion.149), calls=%async_computation.4 | async-start | bytes 2097152 | tf_op jit(solution)/shard_map/all_to_all | solution.py:249
  223.8 1.5 copy-start.7
  223.8 6.9 %copy-start.2 = (bf16[256,8192]{1,0:T(8,128)(2,1)S(1)}, bf16[256,8192]{1,0:T(8,128)(2,1)}, u32[]{:S(2)}) copy-start(bf16[256,8192]{1,0:T(8,128)(2,1)} %maximum_maximum_fusion.1) | copy-start | bytes 12582916
  228.2 5.3 %collective-permute-start = (bf16[128,256]{1,0:T(8,128)(2,1)S(1)}, bf16[128,256]{1,0:T(8,128)(2,1)S(1)}, u32[]{:S(2)}, u32[]{:S(2)}) collective-permute-start(bf16[128,256]{1,0:T(8,128)(2,1)S(1)} %copy_bitcast_fusion.1), channel_id=1, source_target_pairs={{0,1},{1,0},{2,3},{3,2},{4,5},{5,4},{6,7},{7,6},{8,9},{9,8},{10,11... | collective-permute-start | bytes 196616 | tf_op jit(solution)/shard_map/ppermute | solution.py:49
  233.5 1.0 copy-start.3
